TPU v7x, 128 devices: a whole 4x4x4 slice. The times are simulated.
128 devices in a mesh: ctx: 32 (over y, z, core), tp: 4 (over x).
Axes of the slice: x: 4, y: 4, z: 4, core: 2. Of those that a mesh axis runs over, the one named last changes fastest.
Arguments:
- query: bfloat16 [16384, 6144], P('ctx', 'tp'), may hold values from -6 to 6
- key_in: bfloat16 [16384, 6144], P('ctx', 'tp'), may hold values from -6 to 6
- value_in: bfloat16 [16384, 6144], P('ctx', 'tp'), may hold values from -6 to 6
- dout: bfloat16 [16384, 6144], P('ctx', 'tp'), may hold values from -0.5 to 0.5
- summary_offset: int32 [4], replicated, may hold values from 0 to 31
Outputs:
- grad_query: bfloat16 [16384, 6144], P(('ctx', 'tp'))
- grad_key: bfloat16 [16384, 6144], P(('ctx', 'tp'))
- grad_value: bfloat16 [16384, 6144], P(('ctx', 'tp'))
Inputs may be any that keep to these rules, and one draw needn't show every extreme that they name: Summary block s is block s * 32 + summary_offset[s].
All inputs are finite; a program needn't handle non-finite values.
Results may differ from a plain program's by a relative error of at most 0.014.
Values may be sent and summed in bfloat16 or wider, within the bound.
No kernel may reach another device: no remote copies, remote signals or barrier semaphores. Data moves between devices by JAX's collectives and lax.ppermute only.
A program may use at most 128 MiB of HBM per device.

v0:
```python
import jax
import jax.numpy as jnp
from jax import lax
from jax.sharding import PartitionSpec as P

HDIM = 128
BLOCK = 128
BAND = 8
STRIDE = 32
REACH = 2


def passed_along(value, axis, steps):
    count = lax.axis_size(axis)
    leading, last = (max(0, -steps), min(count, count - steps))
    return lax.ppermute(value, axis, [(source, source + steps) for source in range(leading, last)])


def broadcast(value, axis, source):
    kept = jnp.where(lax.axis_index(axis) == source, value, 0).astype(value.dtype)
    return lax.psum(kept, axis)


def band_mask(query_tok, key_tok):
    return (
        (key_tok >= 0)
        & (key_tok <= query_tok)
        & (key_tok // BLOCK >= query_tok // BLOCK - (BAND - 1))
    )


def column(array, start):
    return lax.dynamic_slice_in_dim(array, start, HDIM, 1)


def in_summary(tokens, groups):
    return jnp.any((tokens // BLOCK)[:, None] == groups[None, :], axis=1)


def on_device(query, key_in, value_in, dout, summary_offset):
    rows, width = query.shape
    heads_here = width // HDIM
    me = lax.axis_index("ctx")
    n_ctx = lax.axis_size("ctx")
    scale = HDIM ** (-0.5)
    n_sum = summary_offset.shape[0]
    groups = jnp.arange(n_sum, dtype=jnp.int32) * STRIDE + summary_offset
    owner = groups * BLOCK // rows
    local_start = groups * BLOCK - owner * rows
    within = jnp.arange(BLOCK, dtype=jnp.int32)
    tile_rows = (local_start[:, None] + within[None, :]).reshape(-1)
    sum_tok = (groups[:, None] * BLOCK + within[None, :]).reshape(-1)
    sum_owner = jnp.repeat(owner, BLOCK)
    mine = (sum_owner == me)[:, None]

    def fetch(distance):
        return passed_along((key_in, value_in), "ctx", distance)

    fetched = [fetch(distance) for distance in range(REACH, 0, -1)]
    ext_k = jnp.concatenate([piece[0] for piece in fetched] + [key_in], axis=0)
    ext_v = jnp.concatenate([piece[1] for piece in fetched] + [value_in], axis=0)

    def fill(index, carry):
        start = local_start[index]
        tile = (
            lax.dynamic_slice_in_dim(key_in, start, BLOCK, 0),
            lax.dynamic_slice_in_dim(value_in, start, BLOCK, 0),
        )
        got_k, got_v = (
            broadcast(tile[0], "ctx", owner[index]),
            broadcast(tile[1], "ctx", owner[index]),
        )
        return (
            lax.dynamic_update_slice_in_dim(carry[0], got_k, index * BLOCK, 0),
            lax.dynamic_update_slice_in_dim(carry[1], got_v, index * BLOCK, 0),
        )

    empty = jnp.zeros((n_sum * BLOCK, width), jnp.bfloat16)
    sum_k, sum_v = lax.fori_loop(0, n_sum, fill, (empty, empty))
    key_all = jnp.concatenate([ext_k, sum_k], axis=0)
    value_all = jnp.concatenate([ext_v, sum_v], axis=0)
    query_tok = me * rows + jnp.arange(rows, dtype=jnp.int32)
    ext_tok = (me - REACH) * rows + jnp.arange((REACH + 1) * rows, dtype=jnp.int32)
    elsewhere = in_summary(ext_tok, groups) & (ext_tok < me * rows)
    band_part = (
        band_mask(query_tok[:, None], ext_tok[None, :]) & jnp.logical_not(elsewhere)[None, :]
    )
    sum_block = (sum_tok // BLOCK)[None, :]
    query_block = (query_tok // BLOCK)[:, None]
    before_band = sum_block < query_block - (BAND - 1)
    inside_band = (
        (sum_block >= query_block - (BAND - 1))
        & (sum_block <= query_block)
        & (sum_owner != me)[None, :]
    )
    summary_ok = before_band | inside_band
    allowed = jnp.concatenate([band_part, summary_ok], axis=1)
    first_key = REACH * rows
    kept = key_all.shape[0] - first_key

    def own_head(head, carry):
        grad_q, grad_k, grad_v, lse_all, delta_all = carry
        start = head * HDIM
        rows_q = column(query, start)
        rows_do = column(dout, start)
        keys = column(key_all, start)
        values = column(value_all, start)
        scores = jnp.einsum("qd,kd->qk", rows_q, keys, preferred_element_type=jnp.float32) * scale
        top = jnp.max(jnp.where(allowed, scores, -jnp.inf), axis=1, keepdims=True)
        total = jnp.sum(jnp.where(allowed, jnp.exp(scores - top), 0.0), axis=1, keepdims=True)
        lse = top + jnp.log(total)
        prob = jnp.where(allowed, jnp.exp(scores - lse), 0.0)
        dprob = jnp.einsum("qd,kd->qk", rows_do, values, preferred_element_type=jnp.float32)
        delta = jnp.sum(prob * dprob, axis=1, keepdims=True)
        dscore = (prob * (dprob - delta)).astype(jnp.bfloat16)
        prob_low = prob.astype(jnp.bfloat16)
        head_q = (
            jnp.einsum("qk,kd->qd", dscore, keys, preferred_element_type=jnp.float32) * scale
        ).astype(jnp.bfloat16)
        head_k = (
            jnp.einsum(
                "qk,qd->kd", dscore[:, first_key:], rows_q, preferred_element_type=jnp.float32
            )
            * scale
        )
        head_v = jnp.einsum(
            "qk,qd->kd", prob_low[:, first_key:], rows_do, preferred_element_type=jnp.float32
        )
        grad_q = lax.dynamic_update_slice_in_dim(grad_q, head_q, start, 1)
        grad_k = lax.dynamic_update_slice_in_dim(grad_k, head_k, start, 1)
        grad_v = lax.dynamic_update_slice_in_dim(grad_v, head_v, start, 1)
        lse_all = lax.dynamic_update_slice_in_dim(lse_all, lse.reshape(1, rows), head, 0)
        delta_all = lax.dynamic_update_slice_in_dim(delta_all, delta.reshape(1, rows), head, 0)
        return (grad_q, grad_k, grad_v, lse_all, delta_all)

    start_carry = (
        jnp.zeros((rows, width), jnp.bfloat16),
        jnp.zeros((kept, width), jnp.float32),
        jnp.zeros((kept, width), jnp.float32),
        jnp.zeros((heads_here, rows), jnp.float32),
        jnp.zeros((heads_here, rows), jnp.float32),
    )
    grad_q, grad_k, grad_v, lse_all, delta_all = lax.fori_loop(0, heads_here, own_head, start_carry)

    def remote_terms(later_q, later_do, later_lse, later_delta, later_mask):

        def remote_head(head, carry):
            acc_k, acc_v = carry
            start = head * HDIM
            rows_q = column(later_q, start)
            rows_do = column(later_do, start)
            keys = column(key_in, start)
            values = column(value_in, start)
            lse = lax.dynamic_slice_in_dim(later_lse, head, 1, 0).reshape(rows, 1)
            delta = lax.dynamic_slice_in_dim(later_delta, head, 1, 0).reshape(rows, 1)
            scores = (
                jnp.einsum("qd,kd->qk", rows_q, keys, preferred_element_type=jnp.float32) * scale
            )
            prob = jnp.where(later_mask, jnp.exp(scores - lse), 0.0)
            dprob = jnp.einsum("qd,kd->qk", rows_do, values, preferred_element_type=jnp.float32)
            dscore = (prob * (dprob - delta)).astype(jnp.bfloat16)
            prob_low = prob.astype(jnp.bfloat16)
            head_k = (
                jnp.einsum("qk,qd->kd", dscore, rows_q, preferred_element_type=jnp.float32) * scale
            )
            head_v = jnp.einsum("qk,qd->kd", prob_low, rows_do, preferred_element_type=jnp.float32)
            acc_k = lax.dynamic_update_slice_in_dim(acc_k, column(acc_k, start) + head_k, start, 1)
            acc_v = lax.dynamic_update_slice_in_dim(acc_v, column(acc_v, start) + head_v, start, 1)
            return (acc_k, acc_v)

        return remote_head

    local_k = grad_k[:rows]
    local_v = grad_v[:rows]
    local_tok = me * rows + jnp.arange(rows, dtype=jnp.int32)
    local_plain = jnp.logical_not(in_summary(local_tok, groups))[None, :]
    for distance in range(1, REACH + 1):
        inputs = passed_along((query, dout), "ctx", -distance)
        stats = passed_along((lse_all, delta_all), "ctx", -distance)
        (later_q, later_do), (later_lse, later_delta) = (inputs, stats)
        later_tok = (me + distance) * rows + jnp.arange(rows, dtype=jnp.int32)
        later_mask = (
            band_mask(later_tok[:, None], local_tok[None, :])
            & (later_tok < n_ctx * rows)[:, None]
            & local_plain
        )
        local_k, local_v = lax.fori_loop(
            0,
            heads_here,
            remote_terms(later_q, later_do, later_lse, later_delta, later_mask),
            (local_k, local_v),
        )
    summary_k = grad_k[rows:]
    summary_v = grad_v[rows:]
    total_k, total_v = lax.psum((summary_k, summary_v), "ctx")
    local_k = local_k.at[tile_rows].add(jnp.where(mine, total_k, 0.0))
    local_v = local_v.at[tile_rows].add(jnp.where(mine, total_v, 0.0))
    moved = (
        lax.all_to_all(grad_q, "tp", split_axis=0, concat_axis=1, tiled=True),
        lax.all_to_all(local_k.astype(jnp.bfloat16), "tp", split_axis=0, concat_axis=1, tiled=True),
        lax.all_to_all(local_v.astype(jnp.bfloat16), "tp", split_axis=0, concat_axis=1, tiled=True),
    )
    return (moved[0], moved[1], moved[2])


def solution(mesh):
    return jax.shard_map(
        on_device,
        mesh=mesh,
        in_specs=(P("ctx", "tp"), P("ctx", "tp"), P("ctx", "tp"), P("ctx", "tp"), P()),
        out_specs=(P(("ctx", "tp"), None), P(("ctx", "tp"), None), P(("ctx", "tp"), None)),
        check_vma=False,
    )
```

profile of v0, /device:TPU:8, one launch (start us, length us, event | category | flops | bytes accessed | tf_op | source)
XLA Modules:
  0.0 977.3 jit_solution(13444294860501639880)
XLA Ops:
  8.0 3.8 collective-permute-start
  13.8 3.8 collective-permute-start.2
  21.0 4.3 collective-permute-start.6
  28.9 20.7 %collective-permute-done = bf16[512,1536]{1,0:T(8,128)(2,1)} collective-permute-done((bf16[512,1536]{1,0:T(8,128)(2,1)}, bf16[512,1536]{1,0:T(8,128)(2,1)}, u32[]{:S(2)}, u32[]{:S(2)}) %collective-permute-start) | collective-permute-done | bytes 1572896 | tf_op jit(solution)/shard_map/ppermute | solution.py:16
  49.6 3.7 collective-permute-start.10
  53.3 27.9 %collective-permute-done.1 = bf16[512,1536]{1,0:T(8,128)(2,1)} collective-permute-done((bf16[512,1536]{1,0:T(8,128)(2,1)}, bf16[512,1536]{1,0:T(8,128)(2,1)}, u32[]{:S(2)}, u32[]{:S(2)}) %collective-permute-start.1) | collective-permute-done | bytes 1572896 | tf_op jit(solution)/shard_map/ppermute | solution.py:16
  85.6 458.6 %while.70 = (s32[]{:T(128)}, bf16[512,1536]{1,0:T(8,128)(2,1)}, bf16[512,1536]{1,0:T(8,128)(2,1)}, s32[4]{0:T(128)S(1)}, s32[4]{0:T(128)S(1)}, /*index=5*/bf16[5...) while((s32[]{:T(128)}, bf16[512,1536]{1,0:T(8,128)(2,1)}, ...), condition=%wide.region_3.4_spmd, body=%wide.region_0.3_spmd.sunk | while | flops 786445 | bytes 7864643 | solution.py:79
  91.5 108.0 %all-reduce.9.cloned.1.call-done = (bf16[128,1536]{1,0:T(8,128)(2,1)}, bf16[128,1536]{1,0:T(8,128)(2,1)}) async-done(((bf16[128,1536]{1,0:T(8,128)(2,1)}, bf16[128,1536]{1,0:T(8,128)(2,1)}), (bf16[128,1536]{1,0:T(8,128)(2,1)}, bf16[128,1536]{1,0:T(8,128)(2,1)})) %all-reduce.9.cloned.1.call-update) | async-done | bytes 786448 | tf_op jit(solution)/shard_map/while/body/eval_jaxpr/psum | solution.py:21
  208.9 104.3 %all-reduce.9.cloned.1.call-done = (bf16[128,1536]{1,0:T(8,128)(2,1)}, bf16[128,1536]{1,0:T(8,128)(2,1)}) async-done(((bf16[128,1536]{1,0:T(8,128)(2,1)}, bf16[128,1536]{1,0:T(8,128)(2,1)}), (bf16[128,1536]{1,0:T(8,128)(2,1)}, bf16[128,1536]{1,0:T(8,128)(2,1)})) %all-reduce.9.cloned.1.call-update) | async-done | bytes 786448 | tf_op jit(solution)/shard_map/while/body/eval_jaxpr/psum | solution.py:21
  322.6 104.3 %all-reduce.9.cloned.1.call-done = (bf16[128,1536]{1,0:T(8,128)(2,1)}, bf16[128,1536]{1,0:T(8,128)(2,1)}) async-done(((bf16[128,1536]{1,0:T(8,128)(2,1)}, bf16[128,1536]{1,0:T(8,128)(2,1)}), (bf16[128,1536]{1,0:T(8,128)(2,1)}, bf16[128,1536]{1,0:T(8,128)(2,1)})) %all-reduce.9.cloned.1.call-update) | async-done | bytes 786448 | tf_op jit(solution)/shard_map/while/body/eval_jaxpr/psum | solution.py:21
  436.3 104.3 %all-reduce.9.cloned.1.call-done = (bf16[128,1536]{1,0:T(8,128)(2,1)}, bf16[128,1536]{1,0:T(8,128)(2,1)}) async-done(((bf16[128,1536]{1,0:T(8,128)(2,1)}, bf16[128,1536]{1,0:T(8,128)(2,1)}), (bf16[128,1536]{1,0:T(8,128)(2,1)}, bf16[128,1536]{1,0:T(8,128)(2,1)})) %all-reduce.9.cloned.1.call-update) | async-done | bytes 786448 | tf_op jit(solution)/shard_map/while/body/eval_jaxpr/psum | solution.py:21
  544.2 6.5 pad_maximum_fusion
  550.7 4.9 pad_maximum_fusion.1
  563.6 162.5 %while.71 = (s32[]{:T(128)}, bf16[512,1536]{1,0:T(8,128)(2,1)}, f32[1024,1536]{1,0:T(8,128)}, f32[1024,1536]{1,0:T(8,128)}, f32[12,512]{1,0:T(8,128)S(1)}, /*ind...) while((s32[]{:T(128)}, bf16[512,1536]{1,0:T(8,128)(2,1)}, ...), condition=%wide.region_9.10_spmd, body=%wide.region_5.9_spmd.sunk | while | flops 1089731584 | bytes 42106048 | solution.py:143
  726.1 4.3 collective-permute-start.5
  733.5 6.2 fusion.102
  742.8 4.4 all-to-all-start
  755.6 75.6 %while.72 = (s32[]{:T(128)}, f32[512,1536]{1,0:T(8,128)}, f32[512,1536]{1,0:T(8,128)}, bf16[512,1536]{1,0:T(8,128)(2,1)}, bf16[512,1536]{1,0:T(8,128)(2,1)}, /*i...) while((s32[]{:T(128)}, f32[512,1536]{1,0:T(8,128)}, ...), condition=%wide.region_12.13_spmd.clone, body=%wide.region_11.12_spmd.clone.sunk | while | flops 272039936 | bytes 5007079 | solution.py:187
  831.2 75.5 %while.73 = (s32[]{:T(128)}, f32[512,1536]{1,0:T(8,128)}, f32[512,1536]{1,0:T(8,128)}, bf16[512,1536]{1,0:T(8,128)(2,1)}, bf16[512,1536]{1,0:T(8,128)(2,1)}, /*i...) while((s32[]{:T(128)}, f32[512,1536]{1,0:T(8,128)}, ...), condition=%wide.region_14.15_spmd.clone, body=%wide.region_13.14_spmd.clone.sunk | while | flops 272039936 | bytes 5007079 | solution.py:187
  906.7 10.6 %scatter_custom_fusion.1 = f32[512,1536]{1,0:T(8,128)} fusion(f32[512,1536]{1,0:T(8,128)} %get-tuple-element.718, s32[512]{0:T(512)S(1)} %bitcast.76, f32[512,1536]{1,0:T(8,128)} %get-tuple-element.910, f32[]{:T(128)} %constant.333.clone.1, pred[512]{0:T(512)(128)(4,1)S(1)} %broadcast_bitcast_fusion), kind=kCustom, calls=%fused_computation.91 | custom fusion | flops 1572864 | bytes 6292480 | tf_op jit(solution)/shard_map/scatter-add | solution.py:197
  920.7 4.7 all-to-all-start.2
  925.4 8.2 scatter_custom_fusion
  935.0 10.3 %all-to-all-done.2 = bf16[4,128,1536]{2,1,0:T(8,128)(2,1)} async-done(((bf16[4,128,1536]{2,1,0:T(8,128)(2,1)}), bf16[4,128,1536]{2,1,0:T(8,128)(2,1)}, u32[]{:S(2)}, u32[]{:S(2)}) %all-to-all-start.2) | async-done | bytes 1572896 | tf_op jit(solution)/shard_map/all_to_all | solution.py:201
  955.8 11.9 %all-to-all-done.1 = bf16[4,128,1536]{2,1,0:T(8,128)(2,1)S(1)} async-done(((bf16[4,128,1536]{2,1,0:T(8,128)(2,1)}), bf16[4,128,1536]{2,1,0:T(8,128)(2,1)S(1)}, u32[]{:S(2)}, u32[]{:S(2)}) %all-to-all-start.1) | async-done | bytes 1572896 | tf_op jit(solution)/shard_map/all_to_all | solution.py:200
  (313 shorter events, 393.7 us)
Async XLA Ops:
  8.0 41.6 %collective-permute-start = (bf16[512,1536]{1,0:T(8,128)(2,1)}, bf16[512,1536]{1,0:T(8,128)(2,1)}, u32[]{:S(2)}, u32[]{:S(2)}) collective-permute-start(bf16[512,1536]{1,0:T(8,128)(2,1)} %param.14), channel_id=1, source_target_pairs={{0,8},{4,12},{8,16},{12,20},{16,24},{20,28},{24,32},{28,36},{32,40... | collective-permute-start | bytes 4718600 | tf_op jit(solution)/shard_map/ppermute | solution.py:16
  11.8 69.3 %collective-permute-start.1 = (bf16[512,1536]{1,0:T(8,128)(2,1)}, bf16[512,1536]{1,0:T(8,128)(2,1)}, u32[]{:S(2)}, u32[]{:S(2)}) collective-permute-start(bf16[512,1536]{1,0:T(8,128)(2,1)} %param.14), channel_id=1, source_target_pairs={{0,4},{4,8},{8,12},{12,16},{16,20},{20,24},{24,28},{28,32},{32,36}... | collective-permute-start | bytes 4718600 | tf_op jit(solution)/shard_map/ppermute | solution.py:16
  13.8 536.9 %collective-permute-start.2 = (bf16[512,1536]{1,0:T(8,128)(2,1)}, bf16[512,1536]{1,0:T(8,128)(2,1)}, u32[]{:S(2)}, u32[]{:S(2)}) collective-permute-start(bf16[512,1536]{1,0:T(8,128)(2,1)} %param.15), channel_id=1, source_target_pairs={{0,8},{4,12},{8,16},{12,20},{16,24},{20,28},{24,32},{28,36},{32,40... | collective-permute-start | bytes 4718600 | tf_op jit(solution)/shard_map/ppermute | solution.py:16
  17.6 533.0 %collective-permute-start.3 = (bf16[512,1536]{1,0:T(8,128)(2,1)}, bf16[512,1536]{1,0:T(8,128)(2,1)}, u32[]{:S(2)}, u32[]{:S(2)}) collective-permute-start(bf16[512,1536]{1,0:T(8,128)(2,1)} %param.15), channel_id=1, source_target_pairs={{0,4},{4,8},{8,12},{12,16},{16,20},{20,24},{24,28},{28,32},{32,36}... | collective-permute-start | bytes 4718600 | tf_op jit(solution)/shard_map/ppermute | solution.py:16
  21.0 728.7 %collective-permute-start.6 = (bf16[512,1536]{1,0:T(8,128)(2,1)}, bf16[512,1536]{1,0:T(8,128)(2,1)}, u32[]{:S(2)}, u32[]{:S(2)}) collective-permute-start(bf16[512,1536]{1,0:T(8,128)(2,1)} %param.16), channel_id=1, source_target_pairs={{4,0},{8,4},{12,8},{16,12},{20,16},{24,20},{28,24},{32,28},{36,32}... | collective-permute-start | bytes 4718600 | tf_op jit(solution)/shard_map/ppermute | solution.py:16
  27.3 58.3 %copy-start.2 = (bf16[512,1536]{1,0:T(8,128)(2,1)S(1)}, bf16[512,1536]{1,0:T(8,128)(2,1)}, u32[]{:S(2)}) copy-start(bf16[512,1536]{1,0:T(8,128)(2,1)} %param.15) | copy-start | bytes 4718596
  49.6 781.6 %collective-permute-start.10 = (bf16[512,1536]{1,0:T(8,128)(2,1)}, bf16[512,1536]{1,0:T(8,128)(2,1)}, u32[]{:S(2)}, u32[]{:S(2)}) collective-permute-start(bf16[512,1536]{1,0:T(8,128)(2,1)} %param.16), channel_id=1, source_target_pairs={{8,0},{12,4},{16,8},{20,12},{24,16},{28,20},{32,24},{36,28},{40,32... | collective-permute-start | bytes 4718600 | tf_op jit(solution)/shard_map/ppermute | solution.py:16
  81.2 666.6 %collective-permute-start.4 = (bf16[512,1536]{1,0:T(8,128)(2,1)}, bf16[512,1536]{1,0:T(8,128)(2,1)}, u32[]{:S(2)}, u32[]{:S(2)}) collective-permute-start(bf16[512,1536]{1,0:T(8,128)(2,1)} %param.13), channel_id=1, source_target_pairs={{4,0},{8,4},{12,8},{16,12},{20,16},{24,20},{28,24},{32,28},{36,32}... | collective-permute-start | bytes 4718600 | tf_op jit(solution)/shard_map/ppermute | solution.py:16
  85.6 113.9 %all-reduce.9.cloned.1.call-start = ((), (), s32[]{:S(2)}) async-start(), calls=%async_computation.4 | async-start | bytes 1572864 | tf_op jit(solution)/shard_map/while/body/eval_jaxpr/psum | solution.py:21
  203.0 110.2 %all-reduce.9.cloned.1.call-start = ((), (), s32[]{:S(2)}) async-start(), calls=%async_computation.4 | async-start | bytes 1572864 | tf_op jit(solution)/shard_map/while/body/eval_jaxpr/psum | solution.py:21
  316.7 110.2 %all-reduce.9.cloned.1.call-start = ((), (), s32[]{:S(2)}) async-start(), calls=%async_computation.4 | async-start | bytes 1572864 | tf_op jit(solution)/shard_map/while/body/eval_jaxpr/psum | solution.py:21
  430.5 110.2 %all-reduce.9.cloned.1.call-start = ((), (), s32[]{:S(2)}) async-start(), calls=%async_computation.4 | async-start | bytes 1572864 | tf_op jit(solution)/shard_map/while/body/eval_jaxpr/psum | solution.py:21
  544.2 6.5 copy-start.3
  726.1 26.0 %collective-permute-start.5 = (f32[12,512]{1,0:T(8,128)S(1)}, f32[12,512]{1,0:T(8,128)S(1)}, u32[]{:S(2)}, u32[]{:S(2)}) collective-permute-start(f32[12,512]{1,0:T(8,128)S(1)} %get-tuple-element.713), channel_id=1, source_target_pairs={{4,0},{8,4},{12,8},{16,12},{20,16},{24,20},{28,24},{32,28},{36,32}... | collective-permute-start | bytes 73736 | tf_op jit(solution)/shard_map/ppermute | solution.py:16
  730.4 25.2 %collective-permute-start.7 = (f32[12,512]{1,0:T(8,128)S(1)}, f32[12,512]{1,0:T(8,128)S(1)}, u32[]{:S(2)}, u32[]{:S(2)}) collective-permute-start(f32[12,512]{1,0:T(8,128)S(1)} %get-tuple-element.714), channel_id=1, source_target_pairs={{4,0},{8,4},{12,8},{16,12},{20,16},{24,20},{28,24},{32,28},{36,32}... | collective-permute-start | bytes 73736 | tf_op jit(solution)/shard_map/ppermute | solution.py:16
  733.4 6.3 copy-start.1
  742.8 177.9 %all-to-all-start = ((bf16[4,128,1536]{2,1,0:T(8,128)(2,1)}), bf16[4,128,1536]{2,1,0:T(8,128)(2,1)}, u32[]{:S(2)}, u32[]{:S(2)}) async-start(bf16[4,128,1536]{2,1,0:T(8,128)(2,1)} %bitcast.63), calls=%async_computation | async-start | bytes 3145728 | tf_op jit(solution)/shard_map/all_to_all | solution.py:199
  747.2 159.6 %all-reduce.7.cloned.1.call-start = ((), (), s32[]{:S(2)}) async-start(), calls=%async_computation.3 | async-start | bytes 12582912 | tf_op jit(solution)/shard_map/psum | solution.py:195
  747.8 83.4 %collective-permute-start.8 = (bf16[512,1536]{1,0:T(8,128)(2,1)}, bf16[512,1536]{1,0:T(8,128)(2,1)}, u32[]{:S(2)}, u32[]{:S(2)}) collective-permute-start(bf16[512,1536]{1,0:T(8,128)(2,1)} %param.13), channel_id=1, source_target_pairs={{8,0},{12,4},{16,8},{20,12},{24,16},{28,20},{32,24},{36,28},{40,32... | collective-permute-start | bytes 4718600 | tf_op jit(solution)/shard_map/ppermute | solution.py:16
  749.7 81.5 %collective-permute-start.11 = (f32[12,512]{1,0:T(8,128)S(1)}, f32[12,512]{1,0:T(8,128)S(1)}, u32[]{:S(2)}, u32[]{:S(2)}) collective-permute-start(f32[12,512]{1,0:T(8,128)S(1)} %get-tuple-element.714), channel_id=1, source_target_pairs={{8,0},{12,4},{16,8},{20,12},{24,16},{28,20},{32,24},{36,28},{40,32... | collective-permute-start | bytes 73736 | tf_op jit(solution)/shard_map/ppermute | solution.py:16
  752.1 79.1 %collective-permute-start.9 = (f32[12,512]{1,0:T(8,128)S(1)}, f32[12,512]{1,0:T(8,128)S(1)}, u32[]{:S(2)}, u32[]{:S(2)}) collective-permute-start(f32[12,512]{1,0:T(8,128)S(1)} %get-tuple-element.713), channel_id=1, source_target_pairs={{8,0},{12,4},{16,8},{20,12},{24,16},{28,20},{32,24},{36,28},{40,32... | collective-permute-start | bytes 73736 | tf_op jit(solution)/shard_map/ppermute | solution.py:16
  917.4 8.1 copy-start
  920.7 24.6 %all-to-all-start.2 = ((bf16[4,128,1536]{2,1,0:T(8,128)(2,1)}), bf16[4,128,1536]{2,1,0:T(8,128)(2,1)}, u32[]{:S(2)}, u32[]{:S(2)}) async-start(bf16[4,128,1536]{2,1,0:T(8,128)(2,1)} %bitcast.67), calls=%async_computation.2 | async-start | bytes 3145728 | tf_op jit(solution)/shard_map/all_to_all | solution.py:201
  945.3 22.4 %all-to-all-start.1 = ((bf16[4,128,1536]{2,1,0:T(8,128)(2,1)}), bf16[4,128,1536]{2,1,0:T(8,128)(2,1)S(1)}, u32[]{:S(2)}, u32[]{:S(2)}) async-start(bf16[4,128,1536]{2,1,0:T(8,128)(2,1)} %bitcast.68), calls=%async_computation.1 | async-start | bytes 3145728 | tf_op jit(solution)/shard_map/all_to_all | solution.py:200
Sparse Core Ops, SparseCore 0:
  91.6 107.8 all-reduce.8
  209.0 104.1 all-reduce.8
  322.7 104.1 all-reduce.8
  436.5 104.1 all-reduce.8
Sparse Core Ops, SparseCore 1:
  751.2 130.4 all-reduce.6
where the time goes:
time: 982 us; the launch traced here: 977 us
  waiting for transfers between devices  492 us (50%)
  matrix products  291 us (30%)
  other arithmetic  66.8 us (7%)
  starting transfers between devices  50.7 us (5%)
  local copies, waits for them, and re-layouts  49.6 us (5%)
  between operations  15.5 us (2%)
  loops' own time  11.1 us (1%)
    psum x4, waiting for transfers between devices, broadcast(): return lax.psum(kept, axis)  421 us
    dot_general x24, matrix products, remote_head(): jnp.einsum('qk,qd->kd', dscore, rows_q, preferred_element_type=jnp.float32)  61.8 us
    dot_general x24, matrix products, remote_head(): jnp.einsum('qk,qd->kd', prob_low, rows_do, preferred_element_type=jnp.flo...  50.9 us
    ppermute x12, waiting for transfers between devices, passed_along(): lax.ppermute(value, axis, [(source, source + steps) for source in range(l...  48.6 us
    ppermute x12, starting transfers between devices, passed_along(): lax.ppermute(value, axis, [(source, source + steps) for source in range(l...  38 us
    dot_general x24, matrix products, remote_head(): jnp.einsum('qd,kd->qk', rows_q, keys, preferred_element_type=jnp.float32)  37.9 us
    dot_general x12, matrix products, own_head(): jnp.einsum('qd,kd->qk', rows_do, values, preferred_element_type=jnp.float32)  32.6 us
    dot_general x12, matrix products, own_head(): jnp.einsum('qk,kd->qd', dscore, keys, preferred_element_type=jnp.float32)  28.9 us
  transfers between devices with their start and end apart: 20, of which 8 were waited for; matrix products, arithmetic and copies ran while one was open for 41% of the time, Pallas kernels for 0%

commit v1 on v0

v1 whole, which is shorter than its diff:
```python
import functools
import math

import jax
import jax.numpy as jnp
from jax import lax
from jax.experimental import pallas as pl
from jax.experimental.pallas import tpu as pltpu
from jax.sharding import PartitionSpec as P


HDIM = 128
BLOCK = 128
BAND = 8
STRIDE = 32
CHIP_BLOCKS = 8
HALO = (BAND - 1) * BLOCK
OWN = CHIP_BLOCKS * BLOCK
EXT = HALO + OWN
TILE = 256
NSUM = 4
SPAN = 9
ROWS = (SPAN + NSUM) * BLOCK
NEG = -1e30
SIZES = (2, 2, 2)
BATCHES = ((0, 1), (2,))
CHIPS = 16
SIDE = 4
SCALE = HDIM**-0.5
LOG2E = math.log2(math.e)
BF16 = jnp.bfloat16
F32 = jnp.float32


def ring(step):
    return [(2 * c + k, 2 * ((c + step) % CHIPS) + k) for c in range(CHIPS) for k in range(2)]


def along_z(step):
    return [
        (2 * (y * SIDE + z) + k, 2 * (y * SIDE + (z + step) % SIDE) + k)
        for y in range(SIDE)
        for z in range(SIDE)
        for k in range(2)
    ]


def along_y(step):
    return [
        (2 * (y * SIDE + z) + k, 2 * ((y + step) % SIDE * SIDE + z) + k)
        for y in range(SIDE)
        for z in range(SIDE)
        for k in range(2)
    ]


SWAP = [(d, d ^ 1) for d in range(2 * CHIPS)]


def along_x(step):
    return [(x, (x + step) % SIDE) for x in range(SIDE)]


def params(**kw):
    return pltpu.CompilerParams(vmem_limit_bytes=56 * 1024 * 1024, **kw)


def cost(flops, nbytes):
    return pl.CostEstimate(flops=flops, bytes_accessed=nbytes, transcendentals=0)


def whole(shape):
    return pl.BlockSpec(shape, lambda *_: (0,) * len(shape))


def pack_kernel(sc, off, *refs):
    ins, (own, oth) = refs[:8], refs[8:]
    for n in range(4):
        own[n] = ins[2 * n][...]
        oth[n] = ins[2 * n + 1][...]


def pack(sc, off, arrays, base, heads, width):
    rows = arrays[0].shape[0]
    half = width // HDIM // 2
    chunk = 256
    cols = heads * HDIM
    specs, args = [], []
    for array in arrays:
        for other in (0, 1):
            specs.append(
                pl.BlockSpec(
                    (chunk, cols),
                    lambda i, sc, off, other=other: (
                        i,
                        jnp.abs(sc[1] - other) * (half // heads) + base // heads,
                    ),
                )
            )
            args.append(array)
    out = pl.BlockSpec((4, chunk, cols), lambda i, sc, off: (0, i, 0))
    shape = jax.ShapeDtypeStruct((4, rows, cols), BF16)
    return pl.pallas_call(
        pack_kernel,
        grid_spec=pltpu.PrefetchScalarGridSpec(
            num_scalar_prefetch=2,
            grid=(rows // chunk,),
            in_specs=specs,
            out_specs=[out, out],
        ),
        out_shape=[shape, shape],
        compiler_params=params(),
        cost_estimate=cost(0, 16 * rows * cols * 2),
        name="pack",
    )(sc, off, *args)


def halo_kernel(sc, off, own, recv, out):
    lo = OWN // 2

    def fill(first, second):
        out[:, : lo - BLOCK] = first[:, BLOCK:]
        out[:, lo - BLOCK :] = second[...]

    pl.when(sc[1] == 0)(lambda: fill(own, recv))
    pl.when(sc[1] == 1)(lambda: fill(recv, own))


def halo_of(sc, off, own, recv):
    width = own.shape[2]
    spec = pl.BlockSpec((1, OWN // 2, width), lambda i, sc, off: (2 + i, 0, 0))
    return pl.pallas_call(
        halo_kernel,
        grid_spec=pltpu.PrefetchScalarGridSpec(
            num_scalar_prefetch=2,
            grid=(2,),
            in_specs=[spec, spec],
            out_specs=pl.BlockSpec((1, HALO, width), lambda i, sc, off: (i, 0, 0)),
        ),
        out_shape=jax.ShapeDtypeStruct((2, HALO, width), BF16),
        compiler_params=params(),
        cost_estimate=cost(0, 8 * OWN * width * 2),
        name="halo",
    )(sc, off, own, recv)


def candidate_kernel(sc, off, key, value, own, oth):
    half = own.shape[2]
    for n, ref in enumerate((key, value)):
        own[n] = ref[:, pl.ds(pl.multiple_of(sc[1] * half, HDIM), half)]
        oth[n] = ref[:, pl.ds(pl.multiple_of((1 - sc[1]) * half, HDIM), half)]


def candidate(sc, off, key, value):
    width = key.shape[1]
    spec = pl.BlockSpec((BLOCK, width), lambda i, sc, off: (off[sc[2]] & 3, 0))
    shape = (2, BLOCK, width // 2)
    return pl.pallas_call(
        candidate_kernel,
        grid_spec=pltpu.PrefetchScalarGridSpec(
            num_scalar_prefetch=2, grid=(1,), in_specs=[spec] * 2, out_specs=[whole(shape)] * 2
        ),
        out_shape=[jax.ShapeDtypeStruct(shape, BF16)] * 2,
        compiler_params=params(),
        cost_estimate=cost(0, 8 * BLOCK * width),
        name="candidate",
    )(sc, off, key, value)


def pieces_kernel(sc, off, own, recv, *outs):
    piece = BLOCK // SIDE
    mine = ((off[sc[2]] & 7) >> 2) == sc[1]
    for step in range(SIDE):
        row = pl.multiple_of(((sc[3] + step) & 3) * piece, piece)

        def put(ref, out=outs[step], row=row):
            out[...] = ref[:, pl.ds(row, piece), :]

        pl.when(mine)(functools.partial(put, own))
        pl.when(jnp.logical_not(mine))(functools.partial(put, recv))


def pieces_of(sc, off, own, recv):
    shape = (2, BLOCK // SIDE, own.shape[2])
    return pl.pallas_call(
        pieces_kernel,
        grid_spec=pltpu.PrefetchScalarGridSpec(
            num_scalar_prefetch=2,
            grid=(1,),
            in_specs=[whole(own.shape)] * 2,
            out_specs=[whole(shape)] * SIDE,
        ),
        out_shape=[jax.ShapeDtypeStruct(shape, BF16)] * SIDE,
        compiler_params=params(),
        cost_estimate=cost(0, 8 * own.size),
        name="pieces",
    )(sc, off, own, recv)


def gather_kernel(sc, off, *refs):
    out = refs[SIDE]
    piece = BLOCK // SIDE
    for step in range(SIDE):
        row = pl.multiple_of(((sc[3] + SIDE - step) % SIDE) * piece, piece)
        out[:, pl.ds(row, piece), :] = refs[step][...]


def gather(sc, off, pieces):
    shape = pieces[0].shape
    full = (2, BLOCK, shape[2])
    return pl.pallas_call(
        gather_kernel,
        grid_spec=pltpu.PrefetchScalarGridSpec(
            num_scalar_prefetch=2, grid=(1,), in_specs=[whole(shape)] * SIDE, out_specs=whole(full)
        ),
        out_shape=jax.ShapeDtypeStruct(full, BF16),
        compiler_params=params(),
        cost_estimate=cost(0, 4 * BLOCK * shape[2] * 2),
        name="gather",
    )(sc, off, *pieces)


def fold(x, op):
    return op(x.reshape(x.shape[0] // 8, 8, x.shape[1]), axis=0)


def spread(x):
    return x.reshape(x.shape[0] // 8, 8, x.shape[1])


def dot_nt(a, b):
    return lax.dot_general(a, b, (((1,), (1,)), ((), ())), preferred_element_type=F32)


def dot_nn(a, b):
    return lax.dot_general(a, b, (((1,), (0,)), ((), ())), preferred_element_type=F32)


def attn_kernel(sc, off, own, recv, halo, s0, s1, s2, s3, dq, dkv, dh, ds_out, *scratch):
    kx, vx, qs, dos, kxt, acc_k, acc_v, xs, dps, dsb = scratch
    core, chip, y = sc[1], sc[0], sc[2]
    half = OWN // 2
    mine = pl.multiple_of(core * half, half)
    theirs = pl.multiple_of((1 - core) * half, half)
    qs[pl.ds(mine, half), :] = own[0]
    qs[pl.ds(theirs, half), :] = recv[0]
    dos[pl.ds(mine, half), :] = own[1]
    dos[pl.ds(theirs, half), :] = recv[1]
    for buf, n in ((kx, 0), (vx, 1)):
        buf[0:HALO, :] = halo[n]
        buf[pl.ds(HALO + mine, half), :] = own[2 + n]
        buf[pl.ds(HALO + theirs, half), :] = recv[2 + n]
        for s, part in enumerate((s0, s1, s2, s3)):
            buf[EXT + s * BLOCK : EXT + (s + 1) * BLOCK, :] = part[n]
    kxt[...] = kx[...].T
    acc_k[...] = jnp.zeros_like(acc_k)
    acc_v[...] = jnp.zeros_like(acc_v)
    row = lax.broadcasted_iota(jnp.int32, (BLOCK, TILE), 0)
    col = lax.broadcasted_iota(jnp.int32, (BLOCK, TILE), 1)
    first = lax.broadcasted_iota(jnp.int32, (1, TILE), 1) < BLOCK

    def tile(t, _):
        base = pl.multiple_of(t * TILE, TILE)
        q_t = qs[pl.ds(base, TILE), :]
        do_t = dos[pl.ds(base, TILE), :]

        def rows_of(j):
            if j < SPAN:
                return pl.multiple_of(base + j * BLOCK, BLOCK)
            return EXT + (j - SPAN) * BLOCK

        m8 = jnp.full((8, TILE), NEG, F32)
        l8 = jnp.zeros((8, TILE), F32)
        d8 = jnp.zeros((8, TILE), F32)
        tops = []
        for j in range(SPAN + NSUM):
            span = slice(j * BLOCK, (j + 1) * BLOCK)
            at = pl.ds(rows_of(j), BLOCK)
            x = dot_nt(kx[at, :], q_t) * (SCALE * LOG2E)
            if j < BAND - 1:
                outside = (chip == 0) & (2 * t + j < BAND - 1)
                x = x + jnp.where(outside, NEG, 0.0)
            if j == 0:
                x = jnp.where(first, x, NEG)
            if j == BAND - 1:
                x = jnp.where(row <= col, x, NEG)
            if j == BAND:
                x = jnp.where(row + BLOCK <= col, x, NEG)
            if j >= SPAN:
                slot = (y + NSUM - (j - SPAN)) & 3
                g = slot * STRIDE + off[slot]
                block = chip * CHIP_BLOCKS + 2 * t - (BAND - 1)
                b0 = jnp.where(g < block, 0.0, NEG)
                b1 = jnp.where(g < block + 1, 0.0, NEG)
                x = x + jnp.where(first, b0, b1)
            dp = dot_nt(vx[at, :], do_t)
            top = jnp.maximum(m8, fold(x, jnp.max))
            fade = jnp.exp2(m8 - top)
            p = jnp.exp2(spread(x) - top[None])
            l8 = l8 * fade + jnp.sum(p, axis=0)
            d8 = d8 * fade + jnp.sum(p * spread(dp), axis=0)
            xs[span, :] = p.reshape(BLOCK, TILE)
            dps[span, :] = dp
            m8 = top
            tops.append(top)
        m = jnp.max(m8, axis=0, keepdims=True)
        rest = jnp.exp2(m8 - m)
        inv = 1.0 / jnp.sum(l8 * rest, axis=0, keepdims=True)
        delta = jnp.sum(d8 * rest, axis=0, keepdims=True) * inv
        for j in range(SPAN + NSUM):
            span = slice(j * BLOCK, (j + 1) * BLOCK)
            at = pl.ds(rows_of(j), BLOCK)
            factor = jnp.exp2(tops[j] - m) * inv
            p = (spread(xs[span, :]) * factor[None]).reshape(BLOCK, TILE)
            ds = (p * (dps[span, :] - delta)).astype(BF16)
            dsb[span, :] = ds
            acc_v[at, :] += dot_nn(p.astype(BF16), do_t)
            acc_k[at, :] += dot_nn(ds, q_t)
        dqt = dot_nn(kxt[:, pl.ds(base, SPAN * BLOCK)], dsb[0 : SPAN * BLOCK, :])
        dqt = dqt + dot_nn(kxt[:, EXT:], dsb[SPAN * BLOCK :, :])
        dq[pl.ds(base, TILE), :] = (dqt * SCALE).T.astype(BF16)
        return 0

    lax.fori_loop(0, OWN // TILE, tile, 0)
    dkv[0] = acc_k[HALO:EXT, :] * SCALE
    dkv[1] = acc_v[HALO:EXT, :]
    dh[0] = (acc_k[0:HALO, :] * SCALE).astype(BF16)
    dh[1] = acc_v[0:HALO, :].astype(BF16)
    ds_out[0] = (acc_k[EXT:, :] * SCALE).astype(BF16)
    ds_out[1] = acc_v[EXT:, :].astype(BF16)


def attn(sc, off, own, recv, halo, sums, base):
    width = own.shape[2]
    heads = width // HDIM
    keys = EXT + NSUM * BLOCK

    def by_head(n, rows):
        return pl.BlockSpec((n, rows, HDIM), lambda h, sc, off: (0, 0, h))

    sum_spec = pl.BlockSpec((2, BLOCK, HDIM), lambda h, sc, off: (0, 0, base + h))
    return pl.pallas_call(
        attn_kernel,
        grid_spec=pltpu.PrefetchScalarGridSpec(
            num_scalar_prefetch=2,
            grid=(heads,),
            in_specs=[by_head(4, OWN // 2), by_head(4, OWN // 2), by_head(2, HALO)]
            + [sum_spec] * NSUM,
            out_specs=[
                pl.BlockSpec((OWN, HDIM), lambda h, sc, off: (0, h)),
                by_head(2, OWN),
                by_head(2, HALO),
                by_head(2, NSUM * BLOCK),
            ],
            scratch_shapes=[
                pltpu.VMEM((keys, HDIM), BF16),
                pltpu.VMEM((keys, HDIM), BF16),
                pltpu.VMEM((OWN, HDIM), BF16),
                pltpu.VMEM((OWN, HDIM), BF16),
                pltpu.VMEM((HDIM, keys), BF16),
                pltpu.VMEM((keys, HDIM), F32),
                pltpu.VMEM((keys, HDIM), F32),
                pltpu.VMEM((ROWS, TILE), F32),
                pltpu.VMEM((ROWS, TILE), F32),
                pltpu.VMEM((ROWS, TILE), BF16),
            ],
        ),
        out_shape=[
            jax.ShapeDtypeStruct((OWN, width), BF16),
            jax.ShapeDtypeStruct((2, OWN, width), F32),
            jax.ShapeDtypeStruct((2, HALO, width), BF16),
            jax.ShapeDtypeStruct((2, NSUM * BLOCK, width), BF16),
        ],
        compiler_params=params(),
        cost_estimate=cost(heads * 96 * 10 * 128**3 * 2, heads * 4_000_000),
        name="attn",
    )(sc, off, own, recv, halo, *sums)


def finish_kernel(sc, off, dq, dkv, back, *refs):
    tots, outs = refs[:SIDE], refs[SIDE:]
    core, y, z, x = sc[1], sc[2], sc[3], sc[4]
    local = off[y] & 7
    here = (off[y] >> 3) == z
    total = tots[0][...].astype(F32)
    for part in tots[1:]:
        total = total + part[...].astype(F32)
    for step in range(SIDE):
        for side in range(2):
            block = ((core + side) & 1) * SIDE + ((x + step) & 3)
            rows = pl.ds(pl.multiple_of(block * BLOCK, BLOCK), BLOCK)
            prior = pl.multiple_of(jnp.maximum(block - 1, 0) * BLOCK, BLOCK)
            value = dkv[:, rows, :]
            value = value + jnp.where(block > 0, back[:, pl.ds(prior, BLOCK), :].astype(F32), 0.0)
            value = value + jnp.where(here & (local == block), total, 0.0)
            outs[step][side, 0] = dq[rows, :]
            outs[step][side, 1:3] = value.astype(BF16)


def finish(sc, off, dq, dkv, back, tots, base):
    width = dq.shape[1]
    shape = (2, 3, BLOCK, width)
    return pl.pallas_call(
        finish_kernel,
        grid_spec=pltpu.PrefetchScalarGridSpec(
            num_scalar_prefetch=2,
            grid=(width // HDIM,),
            in_specs=[
                pl.BlockSpec((OWN, HDIM), lambda h, sc, off: (0, h)),
                pl.BlockSpec((2, OWN, HDIM), lambda h, sc, off: (0, 0, h)),
                pl.BlockSpec((2, HALO, HDIM), lambda h, sc, off: (0, 0, h)),
            ]
            + [pl.BlockSpec((2, BLOCK, HDIM), lambda h, sc, off: (0, 0, base + h))] * SIDE,
            out_specs=[pl.BlockSpec((2, 3, BLOCK, HDIM), lambda h, sc, off: (0, 0, 0, h))] * SIDE,
        ),
        out_shape=[jax.ShapeDtypeStruct(shape, BF16)] * SIDE,
        compiler_params=params(),
        cost_estimate=cost(0, 20 * OWN * width),
        name="finish",
    )(sc, off, dq, dkv, back, *tots)


def place_kernel(sc, off, *refs):
    groups = len(SIZES)
    outs = refs[2 * SIDE * groups :]
    x, core = sc[4], sc[1]
    heads = sum(SIZES)
    at = 0
    for g in range(groups):
        width = SIZES[g] * HDIM
        for step in range(SIDE):
            source = (x + SIDE - step) & 3
            for part in range(2):
                side = core if part == 0 else 1 - core
                first = pl.multiple_of(((source * 2 + side) * heads + at) * HDIM, HDIM)
                ref = refs[(g * SIDE + step) * 2 + part]
                for n in range(3):
                    outs[n][:, pl.ds(first, width)] = ref[0, n]
        at += SIZES[g]


def place(sc, off, parts):
    columns = sum(SIZES) * HDIM * 2 * SIDE
    shape = (BLOCK, columns)
    specs = [pl.BlockSpec((1, *p.shape[1:]), lambda i, sc, off: (0, 0, 0, 0)) for p in parts]
    return pl.pallas_call(
        place_kernel,
        grid_spec=pltpu.PrefetchScalarGridSpec(
            num_scalar_prefetch=2,
            grid=(1,),
            in_specs=specs,
            out_specs=[whole(shape)] * 3,
        ),
        out_shape=[jax.ShapeDtypeStruct(shape, BF16)] * 3,
        compiler_params=params(),
        cost_estimate=cost(0, 12 * BLOCK * columns),
        name="place",
    )(sc, off, *parts)


def named(value, pairs, axis="ctx"):
    return lax.ppermute(value, axis, pairs)


def on_device(query, key_in, value_in, dout, off):
    width = query.shape[1]
    me = lax.axis_index("ctx")
    x = lax.axis_index("tp")
    which = lax.iota(jnp.int32, 8)
    sc = jnp.where(which == 0, me >> 1, me & 1)
    sc = jnp.where(which == 2, me >> 3, sc)
    sc = jnp.where(which == 3, (me >> 1) & 3, sc)
    sc = jnp.where(which == 4, x, sc).astype(jnp.int32)
    y, z = me >> 3, (me >> 1) & 3

    own_cand, oth_cand = candidate(sc, off, key_in, value_in)
    pieces = pieces_of(sc, off, own_cand, named(oth_cand, SWAP))
    arrived = [pieces[0]]
    arrived += [named(pieces[n], along_z(n)) for n in range(1, SIDE)]
    step = (z - (off[y] >> 3)) & 3
    piece = arrived[0]
    for n in range(1, SIDE):
        piece = jnp.where(step == n, arrived[n], piece)
    parts = [piece] + [named(piece, along_z(n)) for n in range(1, SIDE)]
    summary = gather(sc, off, parts)
    sums = [summary] + [named(summary, along_y(n)) for n in range(1, SIDE)]

    bases = [sum(SIZES[:g]) for g in range(len(SIZES))]
    owns, recvs, halos = [], [], []
    for g, heads in enumerate(SIZES):
        own, oth = pack(sc, off, (query, dout, key_in, value_in), bases[g], heads, width)
        recv = named(oth, SWAP)
        owns.append(own)
        recvs.append(recv)
        halos.append(named(halo_of(sc, off, own, recv), ring(1)))

    results = [None] * len(SIZES)
    for batch in BATCHES:
        done = []
        for g in batch:
            dq, dkv, dh, dsum = attn(sc, off, owns[g], recvs[g], halos[g], sums, bases[g])
            done.append((dq, dkv, named(dh, ring(-1)), dsum))
        sent = jnp.concatenate([d[3] for d in done], axis=2) if len(done) > 1 else done[0][3]
        part = sent[:, :BLOCK].astype(F32)
        for n in range(1, NSUM):
            moved = named(sent[:, n * BLOCK : (n + 1) * BLOCK], along_y(-n))
            part = part + moved.astype(F32)
        part = part.astype(BF16)
        tots = [part] + [named(part, along_z(n)) for n in range(1, SIDE)]
        for i, g in enumerate(batch):
            dq, dkv, back, _ = done[i]
            cuts = finish(sc, off, dq, dkv, back, tots, bases[g] - bases[batch[0]])
            there = [cuts[0]]
            there += [named(cuts[n], along_x(n), "tp") for n in range(1, SIDE)]
            both = []
            for n in range(SIDE):
                both += [there[n], named(there[n][1:], SWAP)]
            results[g] = both
    return tuple(place(sc, off, [p for both in results for p in both]))


def solution(mesh):
    return jax.shard_map(
        on_device,
        mesh=mesh,
        in_specs=(P("ctx", "tp"), P("ctx", "tp"), P("ctx", "tp"), P("ctx", "tp"), P()),
        out_specs=(P(("ctx", "tp"), None),) * 3,
        check_vma=False,
    )
```

time: 982 us -> 292 us (0.30)
  waiting for transfers between devices: 492 us -> 118 us
  matrix products: 291 us -> 0 us
  Pallas kernels: 0 us -> 98.1 us
  other arithmetic: 66.8 us -> 1.68 us
  local copies, waits for them, and re-layouts: 49.6 us -> 16.1 us
  between operations: 15.5 us -> 1.94 us
  loops' own time: 11.1 us -> 0 us
    psum x5 -> x0, waiting for transfers between devices: 421 us -> none  [the longest x4 421 us: broadcast(): return lax.psum(kept, axis)]
    dot_general x132 -> x0, matrix products: 291 us -> none  [the longest x24 61.8 us: remote_head(): jnp.einsum('qk,qd->kd', dscore, rows_q, preferred_element_type=jnp.float32)]
    pallas_call x0 -> x16, Pallas kernels: none -> 98.1 us  [the longest x3 54.1 us: attn(): pl.pallas_call(attn_kernel, grid_spec=pltpu.PrefetchScalarGridSpec(num_sc...]
    ppermute x12 -> x52, waiting for transfers between devices: 48.6 us -> 118 us  [named(): return lax.ppermute(value, axis, pairs)]
    all_to_all x3 -> x0, waiting for transfers between devices: 22.2 us -> none  [the longest x1 11.9 us: on_device(): lax.all_to_all(local_k.astype(jnp.bfloat16), 'tp', split_axis=0, concat_a...]
    scatter-add x2 -> x0, other arithmetic: 18.8 us -> none  [the longest x1 10.6 us: on_device(): local_v = local_v.at[tile_rows].add(jnp.where(mine, total_v, 0.0))]
    dynamic_update_slice x32 -> x0, local copies, waits for them, and re-layouts: 15.3 us -> none  [the longest x4 7.06 us: fill(): lax.dynamic_update_slice_in_dim(carry[1], got_v, index * BLOCK, 0)]
    reduce_sum x12 -> x0, other arithmetic: 14.7 us -> none  [own_head(): jnp.sum(jnp.where(allowed, jnp.exp(scores - top), 0.0), axis=1, keepdims=...]
  transfers between devices with their start and end apart: 20 -> 52, of which waited for: 8 -> 23; matrix products, arithmetic and copies ran while one was open for 41% -> 3% of each run, Pallas kernels for 0% -> 31%
where the time goes in v1:
time: 292 us; the launch traced here: 287 us
  waiting for transfers between devices  118 us (40%)
  Pallas kernels  98.1 us (34%)
  starting transfers between devices  51.6 us (18%)
  local copies, waits for them, and re-layouts  16.1 us (6%)
    ppermute x52, waiting for transfers between devices, named(): return lax.ppermute(value, axis, pairs)  118 us
    pallas_call x3, Pallas kernels, attn(): pl.pallas_call(attn_kernel, grid_spec=pltpu.PrefetchScalarGridSpec(num_sc...  54.1 us
    ppermute x52, starting transfers between devices, named(): return lax.ppermute(value, axis, pairs)  51.6 us
    pallas_call x3, Pallas kernels, finish(): pl.pallas_call(finish_kernel, grid_spec=pltpu.PrefetchScalarGridSpec(num_...  11.9 us
    pallas_call x3, Pallas kernels, pack(): pl.pallas_call(pack_kernel, grid_spec=pltpu.PrefetchScalarGridSpec(num_sc...  10.4 us
    unnamed x109, local copies, waits for them, and re-layouts  10 us
    pallas_call x3, Pallas kernels, halo_of(): pl.pallas_call(halo_kernel, grid_spec=pltpu.PrefetchScalarGridSpec(num_sc...  8.09 us
    pallas_call x1, Pallas kernels, place(): pl.pallas_call(place_kernel, grid_spec=pltpu.PrefetchScalarGridSpec(num_s...  5.88 us
  transfers between devices with their start and end apart: 52, of which 23 were waited for; matrix products, arithmetic and copies ran while one was open for 3% of the time, Pallas kernels for 31%

profile of v1, /device:TPU:8, one launch (start us, length us, event | category | flops | bytes accessed | tf_op | source)
XLA Modules:
  0.0 287.2 jit_solution(4128273791011345677)
XLA Ops:
  1.2 3.4 %pack.3 = (bf16[4,512,256]{2,1,0:T(8,128)(2,1)}, bf16[4,512,256]{2,1,0:T(8,128)(2,1)}) custom-call(s32[8]{0:T(128)} %compare_select_fusion.3.sc, s32[4]{0:T(128)} %off.31, bf16[512,1536]{1,0:T(8,128)(2,1)} %refs_1_.5, bf16[512,1536]{1,0:T(8,128)(2,1)} %refs_1_.5, bf16[512,1536]{1,0:T(8,128)(2,1)} %refs_3_.5, bf16[512,1536]{1,0:T(8,128)(2,1)} %refs_3_.5, ...), custom_call_target="tpu_custom_call" | custom-call | bytes 4194304 | tf_op jit(solution)/shard_map/pack/pallas_call | solution.py:103
  4.6 3.4 %pack.4 = (bf16[4,512,256]{2,1,0:T(8,128)(2,1)}, bf16[4,512,256]{2,1,0:T(8,128)(2,1)}) custom-call(s32[8]{0:T(128)} %compare_select_fusion.3.sc, s32[4]{0:T(128)} %off.31, bf16[512,1536]{1,0:T(8,128)(2,1)} %refs_1_.5, bf16[512,1536]{1,0:T(8,128)(2,1)} %refs_1_.5, bf16[512,1536]{1,0:T(8,128)(2,1)} %refs_3_.5, bf16[512,1536]{1,0:T(8,128)(2,1)} %refs_3_.5, ...), custom_call_target="tpu_custom_call" | custom-call | bytes 4194304 | tf_op jit(solution)/shard_map/pack/pallas_call | solution.py:103
  11.3 3.5 %pack.5 = (bf16[4,512,256]{2,1,0:T(8,128)(2,1)}, bf16[4,512,256]{2,1,0:T(8,128)(2,1)}) custom-call(s32[8]{0:T(128)} %compare_select_fusion.3.sc, s32[4]{0:T(128)} %off.31, bf16[512,1536]{1,0:T(8,128)(2,1)} %refs_1_.5, bf16[512,1536]{1,0:T(8,128)(2,1)} %refs_1_.5, bf16[512,1536]{1,0:T(8,128)(2,1)} %refs_3_.5, bf16[512,1536]{1,0:T(8,128)(2,1)} %refs_3_.5, ...), custom_call_target="tpu_custom_call" | custom-call | bytes 4194304 | tf_op jit(solution)/shard_map/pack/pallas_call | solution.py:103
  18.6 4.1 %collective-permute-start.3 = (bf16[2,32,768]{2,1,0:T(8,128)(2,1)}, bf16[2,32,768]{2,1,0:T(8,128)(2,1)S(1)}, u32[]{:S(2)}, u32[]{:S(2)}) collective-permute-start(bf16[2,32,768]{2,1,0:T(8,128)(2,1)} %get-tuple-element.43), channel_id=1, source_target_pairs={{0,24},{4,28},{8,0},{12,4},{16,8},{20,12},{24,16},{28,20},{32,56},... | collective-permute-start | bytes 294920 | tf_op jit(solution)/shard_map/ppermute | solution.py:462
  31.3 3.2 %collective-permute-start.7 = (bf16[2,32,768]{2,1,0:T(8,128)(2,1)S(1)}, bf16[2,32,768]{2,1,0:T(8,128)(2,1)S(1)}, u32[]{:S(2)}, u32[]{:S(2)}) collective-permute-start(bf16[2,32,768]{2,1,0:T(8,128)(2,1)S(1)} %select_select_fusion.refs_0_), channel_id=1, source_target_pairs={{0,16},{4,20},{8,24},{12,28},{16,0},{20,4},{24,8},{28,12},{32,48},... | collective-permute-start | bytes 294920 | tf_op jit(solution)/shard_map/ppermute | solution.py:462
  34.5 19.3 %collective-permute-done.6.refs_1_ = bf16[2,32,768]{2,1,0:T(8,128)(2,1)S(1)} collective-permute-done((bf16[2,32,768]{2,1,0:T(8,128)(2,1)S(1)}, bf16[2,32,768]{2,1,0:T(8,128)(2,1)S(1)}, u32[]{:S(2)}, u32[]{:S(2)}) %collective-permute-start.6) | collective-permute-done | bytes 98336 | tf_op jit(solution)/shard_map/ppermute | solution.py:462
  63.2 5.2 %collective-permute-start.10 = (bf16[2,128,768]{2,1,0:T(8,128)(2,1)}, bf16[2,128,768]{2,1,0:T(8,128)(2,1)S(1)}, u32[]{:S(2)}, u32[]{:S(2)}) collective-permute-start(bf16[2,128,768]{2,1,0:T(8,128)(2,1)} %gather.1.s0), channel_id=1, source_target_pairs={{0,64},{4,68},{8,72},{12,76},{16,80},{20,84},{24,88},{28,92},{32,9... | collective-permute-start | bytes 1179656 | tf_op jit(solution)/shard_map/ppermute | solution.py:462
  78.6 6.6 %collective-permute-done.11.s3 = bf16[2,128,768]{2,1,0:T(8,128)(2,1)S(1)} collective-permute-done((bf16[2,128,768]{2,1,0:T(8,128)(2,1)}, bf16[2,128,768]{2,1,0:T(8,128)(2,1)S(1)}, u32[]{:S(2)}, u32[]{:S(2)}) %collective-permute-start.11) | collective-permute-done | bytes 393248 | tf_op jit(solution)/shard_map/ppermute | solution.py:462
  86.9 18.1 %attn.3 = (bf16[1024,256]{1,0:T(8,128)(2,1)}, f32[2,1024,256]{2,1,0:T(8,128)}, bf16[2,896,256]{2,1,0:T(8,128)(2,1)}, bf16[2,512,256]{2,1,0:T(8,128)(2,1)}) custom-call(s32[8]{0:T(128)} %compare_select_fusion.3.sc, s32[4]{0:T(128)} %off.31, bf16[4,512,256]{2,1,0:T(8,128)(2,1)} %get-tuple-element.39.own, bf16[4,512,256]{2,1,0:T(8,128)(2,1)} %copy-done.6, ...), custom_call_target="tpu_custom_call" | custom-call | flops 8053063680 | bytes 8000000 | tf_op jit(solution)/shard_map/attn/pallas_call | solution.py:342
  104.9 3.9 %collective-permute-start.12 = (bf16[2,896,256]{2,1,0:T(8,128)(2,1)}, bf16[2,896,256]{2,1,0:T(8,128)(2,1)S(1)}, u32[]{:S(2)}, u32[]{:S(2)}) collective-permute-start(bf16[2,896,256]{2,1,0:T(8,128)(2,1)} %get-tuple-element.49), channel_id=1, source_target_pairs={{0,120},{4,124},{8,0},{12,4},{16,8},{20,12},{24,16},{28,20},{32,24... | collective-permute-start | bytes 2752520 | tf_op jit(solution)/shard_map/ppermute | solution.py:462
  110.8 18.0 %attn.4 = (bf16[1024,256]{1,0:T(8,128)(2,1)}, f32[2,1024,256]{2,1,0:T(8,128)}, bf16[2,896,256]{2,1,0:T(8,128)(2,1)}, bf16[2,512,256]{2,1,0:T(8,128)(2,1)}) custom-call(s32[8]{0:T(128)} %compare_select_fusion.3.sc, s32[4]{0:T(128)} %off.31, bf16[4,512,256]{2,1,0:T(8,128)(2,1)} %get-tuple-element.51.own, bf16[4,512,256]{2,1,0:T(8,128)(2,1)} %copy-done.5, ...), custom_call_target="tpu_custom_call" | custom-call | flops 8053063680 | bytes 8000000 | tf_op jit(solution)/shard_map/attn/pallas_call | solution.py:342
  130.2 5.0 %collective-permute-start.16 = (bf16[2,128,512]{2,1,0:T(8,128)(2,1)S(1)}, bf16[2,128,512]{2,1,0:T(8,128)(2,1)S(1)}, u32[]{:S(2)}, u32[]{:S(2)}) collective-permute-start(bf16[2,128,512]{2,1,0:T(8,128)(2,1)S(1)} %get-tuple-element.77), channel_id=1, source_target_pairs={{0,64},{4,68},{8,72},{12,76},{16,80},{20,84},{24,88},{28,92},{32,9... | collective-permute-start | bytes 786440 | tf_op jit(solution)/shard_map/ppermute | solution.py:462
  136.1 18.0 %attn.5 = (bf16[1024,256]{1,0:T(8,128)(2,1)}, f32[2,1024,256]{2,1,0:T(8,128)}, bf16[2,896,256]{2,1,0:T(8,128)(2,1)}, bf16[2,512,256]{2,1,0:T(8,128)(2,1)}) custom-call(s32[8]{0:T(128)} %compare_select_fusion.3.sc, s32[4]{0:T(128)} %off.31, bf16[4,512,256]{2,1,0:T(8,128)(2,1)} %get-tuple-element.65.own, bf16[4,512,256]{2,1,0:T(8,128)(2,1)} %copy-done.4, ...), custom_call_target="tpu_custom_call" | custom-call | flops 8053063680 | bytes 8000000 | tf_op jit(solution)/shard_map/attn/pallas_call | solution.py:342
  162.3 31.4 %collective-permute-done.40 = bf16[2,128,256]{2,1,0:T(8,128)(2,1)S(1)} collective-permute-done((bf16[2,128,256]{2,1,0:T(8,128)(2,1)S(1)}, bf16[2,128,256]{2,1,0:T(8,128)(2,1)S(1)}, u32[]{:S(2)}, u32[]{:S(2)}) %collective-permute-start.40) | collective-permute-done | bytes 131104 | tf_op jit(solution)/shard_map/ppermute | solution.py:462
  193.6 5.0 %collective-permute-done.39 = bf16[2,128,256]{2,1,0:T(8,128)(2,1)S(1)} collective-permute-done((bf16[2,128,256]{2,1,0:T(8,128)(2,1)S(1)}, bf16[2,128,256]{2,1,0:T(8,128)(2,1)S(1)}, u32[]{:S(2)}, u32[]{:S(2)}) %collective-permute-start.39) | collective-permute-done | bytes 131104 | tf_op jit(solution)/shard_map/ppermute | solution.py:462
  199.7 8.3 %collective-permute-done.19.refs_2_ = bf16[2,128,512]{2,1,0:T(8,128)(2,1)S(1)} collective-permute-done((bf16[2,128,512]{2,1,0:T(8,128)(2,1)S(1)}, bf16[2,128,512]{2,1,0:T(8,128)(2,1)S(1)}, u32[]{:S(2)}, u32[]{:S(2)}) %collective-permute-start.19) | collective-permute-done | bytes 262176 | tf_op jit(solution)/shard_map/ppermute | solution.py:462
  211.8 3.9 %finish.3 = (bf16[2,3,128,256]{3,2,1,0:T(8,128)(2,1)}, bf16[2,3,128,256]{3,2,1,0:T(8,128)(2,1)}, bf16[2,3,128,256]{3,2,1,0:T(8,128)(2,1)}, bf16[2,3,128,256]{3,2,1,0:T(8,128)(2,1)}) custom-call(s32[8]{0:T(128)} %compare_select_fusion.3.sc, s32[4]{0:T(128)} %off.31, bf16[1024,256]{1,0:T(8,128)(2,1)} %get-tuple-element.47.dq, ...), custom_call_target="tpu_custom_call" | custom-call | bytes 5242880 | tf_op jit(solution)/shard_map/finish/pallas_call | solution.py:403
  217.6 4.0 %finish.4 = (bf16[2,3,128,256]{3,2,1,0:T(8,128)(2,1)}, bf16[2,3,128,256]{3,2,1,0:T(8,128)(2,1)}, bf16[2,3,128,256]{3,2,1,0:T(8,128)(2,1)}, bf16[2,3,128,256]{3,2,1,0:T(8,128)(2,1)}) custom-call(s32[8]{0:T(128)} %compare_select_fusion.3.sc, s32[4]{0:T(128)} %off.31, bf16[1024,256]{1,0:T(8,128)(2,1)} %get-tuple-element.58.dq, ...), custom_call_target="tpu_custom_call" | custom-call | bytes 5242880 | tf_op jit(solution)/shard_map/finish/pallas_call | solution.py:403
  229.2 3.9 %finish.5 = (bf16[2,3,128,256]{3,2,1,0:T(8,128)(2,1)}, bf16[2,3,128,256]{3,2,1,0:T(8,128)(2,1)}, bf16[2,3,128,256]{3,2,1,0:T(8,128)(2,1)}, bf16[2,3,128,256]{3,2,1,0:T(8,128)(2,1)}) custom-call(s32[8]{0:T(128)} %compare_select_fusion.3.sc, s32[4]{0:T(128)} %off.31, bf16[1024,256]{1,0:T(8,128)(2,1)} %get-tuple-element.67.dq, ...), custom_call_target="tpu_custom_call" | custom-call | bytes 5242880 | tf_op jit(solution)/shard_map/finish/pallas_call | solution.py:403
  234.5 7.8 %collective-permute-done.22.refs_2_ = bf16[2,3,128,256]{3,2,1,0:T(8,128)(2,1)S(1)} collective-permute-done((bf16[2,3,128,256]{3,2,1,0:T(8,128)(2,1)S(1)}, bf16[2,3,128,256]{3,2,1,0:T(8,128)(2,1)S(1)}, u32[]{:S(2)}, u32[]{:S(2)}) %collective-permute-start.22) | collective-permute-done | bytes 393248 | tf_op jit(solution)/shard_map/ppermute | solution.py:462
  247.3 11.8 %collective-permute-done.30.refs_10_ = bf16[2,3,128,256]{3,2,1,0:T(8,128)(2,1)S(1)} collective-permute-done((bf16[2,3,128,256]{3,2,1,0:T(8,128)(2,1)}, bf16[2,3,128,256]{3,2,1,0:T(8,128)(2,1)S(1)}, u32[]{:S(2)}, u32[]{:S(2)}) %collective-permute-start.30) | collective-permute-done | bytes 393248 | tf_op jit(solution)/shard_map/ppermute | solution.py:462
  261.8 5.8 %collective-permute-done.46.refs_18_ = bf16[2,3,128,256]{3,2,1,0:T(8,128)(2,1)S(1)} collective-permute-done((bf16[2,3,128,256]{3,2,1,0:T(8,128)(2,1)}, bf16[2,3,128,256]{3,2,1,0:T(8,128)(2,1)S(1)}, u32[]{:S(2)}, u32[]{:S(2)}) %collective-permute-start.46) | collective-permute-done | bytes 393248 | tf_op jit(solution)/shard_map/ppermute | solution.py:462
  267.6 9.3 %collective-permute-done.48.refs_20_ = bf16[2,3,128,256]{3,2,1,0:T(8,128)(2,1)S(1)} collective-permute-done((bf16[2,3,128,256]{3,2,1,0:T(8,128)(2,1)}, bf16[2,3,128,256]{3,2,1,0:T(8,128)(2,1)S(1)}, u32[]{:S(2)}, u32[]{:S(2)}) %collective-permute-start.48) | collective-permute-done | bytes 393248 | tf_op jit(solution)/shard_map/ppermute | solution.py:462
  281.3 5.9 %place.1 = (bf16[128,6144]{1,0:T(8,128)(2,1)}, bf16[128,6144]{1,0:T(8,128)(2,1)}, bf16[128,6144]{1,0:T(8,128)(2,1)}) custom-call(s32[8]{0:T(128)} %compare_select_fusion.3.sc, s32[4]{0:T(128)} %off.31, bf16[2,3,128,256]{3,2,1,0:T(8,128)(2,1)} %get-tuple-element.54.refs_0_, bf16[1,3,128,256]{3,2,1,0:T(8,128)(2,1)} %copy-done.22, ...), custom_call_target="tpu_custom_call" | custom-call | bytes 9437184 | tf_op jit(solution)/shard_map/place/pallas_call | solution.py:446
  (225 shorter events, 76.6 us)
Async XLA Ops:
  4.6 18.1 %collective-permute-start = (bf16[4,512,256]{2,1,0:T(8,128)(2,1)}, bf16[4,512,256]{2,1,0:T(8,128)(2,1)S(1)}, u32[]{:S(2)}, u32[]{:S(2)}) collective-permute-start(bf16[4,512,256]{2,1,0:T(8,128)(2,1)} %get-tuple-element.40), channel_id=1, source_target_pairs={{0,4},{4,0},{8,12},{12,8},{16,20},{20,16},{24,28},{28,24},{32,36},... | collective-permute-start | bytes 3145736 | tf_op jit(solution)/shard_map/ppermute | solution.py:462
  8.0 60.3 %collective-permute-start.13 = (bf16[4,512,256]{2,1,0:T(8,128)(2,1)}, bf16[4,512,256]{2,1,0:T(8,128)(2,1)S(1)}, u32[]{:S(2)}, u32[]{:S(2)}) collective-permute-start(bf16[4,512,256]{2,1,0:T(8,128)(2,1)} %get-tuple-element.52), channel_id=1, source_target_pairs={{0,4},{4,0},{8,12},{12,8},{16,20},{20,16},{24,28},{28,24},{32,36},... | collective-permute-start | bytes 3145736 | tf_op jit(solution)/shard_map/ppermute | solution.py:462
  14.8 57.2 %collective-permute-start.36 = (bf16[4,512,256]{2,1,0:T(8,128)(2,1)}, bf16[4,512,256]{2,1,0:T(8,128)(2,1)S(1)}, u32[]{:S(2)}, u32[]{:S(2)}) collective-permute-start(bf16[4,512,256]{2,1,0:T(8,128)(2,1)} %get-tuple-element.66), channel_id=1, source_target_pairs={{0,4},{4,0},{8,12},{12,8},{16,20},{20,16},{24,28},{28,24},{32,36},... | collective-permute-start | bytes 3145736 | tf_op jit(solution)/shard_map/ppermute | solution.py:462
  27.4 57.8 %collective-permute-start.1 = (bf16[2,896,256]{2,1,0:T(8,128)(2,1)}, bf16[2,896,256]{2,1,0:T(8,128)(2,1)S(1)}, u32[]{:S(2)}, u32[]{:S(2)}) collective-permute-start(bf16[2,896,256]{2,1,0:T(8,128)(2,1)} %halo.3), channel_id=1, source_target_pairs={{0,8},{4,12},{8,16},{12,20},{16,24},{20,28},{24,32},{28,36},{32,40... | collective-permute-start | bytes 2752520 | tf_op jit(solution)/shard_map/ppermute | solution.py:462
  30.8 23.0 %collective-permute-start.6 = (bf16[2,32,768]{2,1,0:T(8,128)(2,1)S(1)}, bf16[2,32,768]{2,1,0:T(8,128)(2,1)S(1)}, u32[]{:S(2)}, u32[]{:S(2)}) collective-permute-start(bf16[2,32,768]{2,1,0:T(8,128)(2,1)S(1)} %select_select_fusion.refs_0_), channel_id=1, source_target_pairs={{0,8},{4,12},{8,16},{12,20},{16,24},{20,28},{24,0},{28,4},{32,40},... | collective-permute-start | bytes 294920 | tf_op jit(solution)/shard_map/ppermute | solution.py:462
  31.3 25.4 %collective-permute-start.7 = (bf16[2,32,768]{2,1,0:T(8,128)(2,1)S(1)}, bf16[2,32,768]{2,1,0:T(8,128)(2,1)S(1)}, u32[]{:S(2)}, u32[]{:S(2)}) collective-permute-start(bf16[2,32,768]{2,1,0:T(8,128)(2,1)S(1)} %select_select_fusion.refs_0_), channel_id=1, source_target_pairs={{0,16},{4,20},{8,24},{12,28},{16,0},{20,4},{24,8},{28,12},{32,48},... | collective-permute-start | bytes 294920 | tf_op jit(solution)/shard_map/ppermute | solution.py:462
  72.0 37.9 %collective-permute-start.14 = (bf16[2,896,256]{2,1,0:T(8,128)(2,1)}, bf16[2,896,256]{2,1,0:T(8,128)(2,1)S(1)}, u32[]{:S(2)}, u32[]{:S(2)}) collective-permute-start(bf16[2,896,256]{2,1,0:T(8,128)(2,1)} %halo.4), channel_id=1, source_target_pairs={{0,8},{4,12},{8,16},{12,20},{16,24},{20,28},{24,32},{28,36},{32,40... | collective-permute-start | bytes 2752520 | tf_op jit(solution)/shard_map/ppermute | solution.py:462
  76.5 58.7 %collective-permute-start.37 = (bf16[2,896,256]{2,1,0:T(8,128)(2,1)}, bf16[2,896,256]{2,1,0:T(8,128)(2,1)S(1)}, u32[]{:S(2)}, u32[]{:S(2)}) collective-permute-start(bf16[2,896,256]{2,1,0:T(8,128)(2,1)} %halo.5), channel_id=1, source_target_pairs={{0,8},{4,12},{8,16},{12,20},{16,24},{20,28},{24,32},{28,36},{32,40... | collective-permute-start | bytes 2752520 | tf_op jit(solution)/shard_map/ppermute | solution.py:462
  104.9 105.9 %collective-permute-start.12 = (bf16[2,896,256]{2,1,0:T(8,128)(2,1)}, bf16[2,896,256]{2,1,0:T(8,128)(2,1)S(1)}, u32[]{:S(2)}, u32[]{:S(2)}) collective-permute-start(bf16[2,896,256]{2,1,0:T(8,128)(2,1)} %get-tuple-element.49), channel_id=1, source_target_pairs={{0,120},{4,124},{8,0},{12,4},{16,8},{20,12},{24,16},{28,20},{32,24... | collective-permute-start | bytes 2752520 | tf_op jit(solution)/shard_map/ppermute | solution.py:462
  130.1 24.0 %collective-permute-start.17 = (bf16[2,128,512]{2,1,0:T(8,128)(2,1)S(1)}, bf16[2,128,512]{2,1,0:T(8,128)(2,1)S(1)}, u32[]{:S(2)}, u32[]{:S(2)}) collective-permute-start(bf16[2,128,512]{2,1,0:T(8,128)(2,1)S(1)} %get-tuple-element.76), channel_id=1, source_target_pairs={{0,32},{4,36},{8,40},{12,44},{16,48},{20,52},{24,56},{28,60},{32,6... | collective-permute-start | bytes 786440 | tf_op jit(solution)/shard_map/ppermute | solution.py:462
  130.2 25.2 %collective-permute-start.16 = (bf16[2,128,512]{2,1,0:T(8,128)(2,1)S(1)}, bf16[2,128,512]{2,1,0:T(8,128)(2,1)S(1)}, u32[]{:S(2)}, u32[]{:S(2)}) collective-permute-start(bf16[2,128,512]{2,1,0:T(8,128)(2,1)S(1)} %get-tuple-element.77), channel_id=1, source_target_pairs={{0,64},{4,68},{8,72},{12,76},{16,80},{20,84},{24,88},{28,92},{32,9... | collective-permute-start | bytes 786440 | tf_op jit(solution)/shard_map/ppermute | solution.py:462
  135.1 22.2 %collective-permute-start.15 = (bf16[2,128,512]{2,1,0:T(8,128)(2,1)S(1)}, bf16[2,128,512]{2,1,0:T(8,128)(2,1)S(1)}, u32[]{:S(2)}, u32[]{:S(2)}) collective-permute-start(bf16[2,128,512]{2,1,0:T(8,128)(2,1)S(1)} %get-tuple-element.75), channel_id=1, source_target_pairs={{0,96},{4,100},{8,104},{12,108},{16,112},{20,116},{24,120},{28,124... | collective-permute-start | bytes 786440 | tf_op jit(solution)/shard_map/ppermute | solution.py:462
  135.1 81.5 %collective-permute-start.28 = (bf16[2,896,256]{2,1,0:T(8,128)(2,1)S(1)}, bf16[2,896,256]{2,1,0:T(8,128)(2,1)S(1)}, u32[]{:S(2)}, u32[]{:S(2)}) collective-permute-start(bf16[2,896,256]{2,1,0:T(8,128)(2,1)S(1)} %copy-done.42), channel_id=1, source_target_pairs={{0,120},{4,124},{8,0},{12,4},{16,8},{20,12},{24,16},{28,20},{32,24... | collective-permute-start | bytes 2752520 | tf_op jit(solution)/shard_map/ppermute | solution.py:462
  154.1 73.5 %collective-permute-start.38 = (bf16[2,896,256]{2,1,0:T(8,128)(2,1)}, bf16[2,896,256]{2,1,0:T(8,128)(2,1)S(1)}, u32[]{:S(2)}, u32[]{:S(2)}) collective-permute-start(bf16[2,896,256]{2,1,0:T(8,128)(2,1)} %get-tuple-element.69), channel_id=1, source_target_pairs={{0,120},{4,124},{8,0},{12,4},{16,8},{20,12},{24,16},{28,20},{32,24... | collective-permute-start | bytes 2752520 | tf_op jit(solution)/shard_map/ppermute | solution.py:462
  157.3 36.3 %collective-permute-start.40 = (bf16[2,128,256]{2,1,0:T(8,128)(2,1)S(1)}, bf16[2,128,256]{2,1,0:T(8,128)(2,1)S(1)}, u32[]{:S(2)}, u32[]{:S(2)}) collective-permute-start(bf16[2,128,256]{2,1,0:T(8,128)(2,1)S(1)} %get-tuple-element.80), channel_id=1, source_target_pairs={{0,64},{4,68},{8,72},{12,76},{16,80},{20,84},{24,88},{28,92},{32,9... | collective-permute-start | bytes 393224 | tf_op jit(solution)/shard_map/ppermute | solution.py:462
  160.4 38.2 %collective-permute-start.18 = (bf16[2,128,512]{2,1,0:T(8,128)(2,1)S(1)}, bf16[2,128,512]{2,1,0:T(8,128)(2,1)S(1)}, u32[]{:S(2)}, u32[]{:S(2)}) collective-permute-start(bf16[2,128,512]{2,1,0:T(8,128)(2,1)S(1)} %add_convert_fusion.refs_0_), channel_id=1, source_target_pairs={{0,8},{4,12},{8,16},{12,20},{16,24},{20,28},{24,0},{28,4},{32,40},... | collective-permute-start | bytes 786440 | tf_op jit(solution)/shard_map/ppermute | solution.py:462
  221.7 20.7 %collective-permute-start.22 = (bf16[2,3,128,256]{3,2,1,0:T(8,128)(2,1)S(1)}, bf16[2,3,128,256]{3,2,1,0:T(8,128)(2,1)S(1)}, u32[]{:S(2)}, u32[]{:S(2)}) collective-permute-start(bf16[2,3,128,256]{3,2,1,0:T(8,128)(2,1)S(1)} %copy-done.53), channel_id=1, source_target_pairs={{0,1},{1,2},{2,3},{3,0},{4,5},{5,6},{6,7},{7,4},{8,9},{9,10},{10,1... | collective-permute-start | bytes 1179656 | tf_op jit(solution)/shard_map/ppermute | solution.py:462
  223.2 21.2 %collective-permute-start.24 = (bf16[2,3,128,256]{3,2,1,0:T(8,128)(2,1)S(1)}, bf16[2,3,128,256]{3,2,1,0:T(8,128)(2,1)S(1)}, u32[]{:S(2)}, u32[]{:S(2)}) collective-permute-start(bf16[2,3,128,256]{3,2,1,0:T(8,128)(2,1)S(1)} %copy-done.51), channel_id=1, source_target_pairs={{0,2},{1,3},{2,0},{3,1},{4,6},{5,7},{6,4},{7,5},{8,10},{9,11},{10,... | collective-permute-start | bytes 1179656 | tf_op jit(solution)/shard_map/ppermute | solution.py:462
  226.0 18.4 %collective-permute-start.26 = (bf16[2,3,128,256]{3,2,1,0:T(8,128)(2,1)S(1)}, bf16[2,3,128,256]{3,2,1,0:T(8,128)(2,1)S(1)}, u32[]{:S(2)}, u32[]{:S(2)}) collective-permute-start(bf16[2,3,128,256]{3,2,1,0:T(8,128)(2,1)S(1)} %copy-done.49), channel_id=1, source_target_pairs={{0,3},{1,0},{2,1},{3,2},{4,7},{5,4},{6,5},{7,6},{8,11},{9,8},{10,9... | collective-permute-start | bytes 1179656 | tf_op jit(solution)/shard_map/ppermute | solution.py:462
  227.6 31.6 %collective-permute-start.30 = (bf16[2,3,128,256]{3,2,1,0:T(8,128)(2,1)}, bf16[2,3,128,256]{3,2,1,0:T(8,128)(2,1)S(1)}, u32[]{:S(2)}, u32[]{:S(2)}) collective-permute-start(bf16[2,3,128,256]{3,2,1,0:T(8,128)(2,1)} %get-tuple-element.62), channel_id=1, source_target_pairs={{0,1},{1,2},{2,3},{3,0},{4,5},{5,6},{6,7},{7,4},{8,9},{9,10},{10,1... | collective-permute-start | bytes 1179656 | tf_op jit(solution)/shard_map/ppermute | solution.py:462
  233.2 28.0 %collective-permute-start.32 = (bf16[2,3,128,256]{3,2,1,0:T(8,128)(2,1)S(1)}, bf16[2,3,128,256]{3,2,1,0:T(8,128)(2,1)S(1)}, u32[]{:S(2)}, u32[]{:S(2)}) collective-permute-start(bf16[2,3,128,256]{3,2,1,0:T(8,128)(2,1)S(1)} %copy-done.47), channel_id=1, source_target_pairs={{0,2},{1,3},{2,0},{3,1},{4,6},{5,7},{6,4},{7,5},{8,10},{9,11},{10,... | collective-permute-start | bytes 1179656 | tf_op jit(solution)/shard_map/ppermute | solution.py:462
  242.3 19.0 %collective-permute-start.34 = (bf16[2,3,128,256]{3,2,1,0:T(8,128)(2,1)S(1)}, bf16[2,3,128,256]{3,2,1,0:T(8,128)(2,1)S(1)}, u32[]{:S(2)}, u32[]{:S(2)}) collective-permute-start(bf16[2,3,128,256]{3,2,1,0:T(8,128)(2,1)S(1)} %copy-done.46), channel_id=1, source_target_pairs={{0,3},{1,0},{2,1},{3,2},{4,7},{5,4},{6,5},{7,6},{8,11},{9,8},{10,9... | collective-permute-start | bytes 1179656 | tf_op jit(solution)/shard_map/ppermute | solution.py:462
  244.4 23.2 %collective-permute-start.46 = (bf16[2,3,128,256]{3,2,1,0:T(8,128)(2,1)}, bf16[2,3,128,256]{3,2,1,0:T(8,128)(2,1)S(1)}, u32[]{:S(2)}, u32[]{:S(2)}) collective-permute-start(bf16[2,3,128,256]{3,2,1,0:T(8,128)(2,1)} %get-tuple-element.72), channel_id=1, source_target_pairs={{0,1},{1,2},{2,3},{3,0},{4,5},{5,6},{6,7},{7,4},{8,9},{9,10},{10,1... | collective-permute-start | bytes 1179656 | tf_op jit(solution)/shard_map/ppermute | solution.py:462
  244.4 32.4 %collective-permute-start.48 = (bf16[2,3,128,256]{3,2,1,0:T(8,128)(2,1)}, bf16[2,3,128,256]{3,2,1,0:T(8,128)(2,1)S(1)}, u32[]{:S(2)}, u32[]{:S(2)}) collective-permute-start(bf16[2,3,128,256]{3,2,1,0:T(8,128)(2,1)} %get-tuple-element.73), channel_id=1, source_target_pairs={{0,2},{1,3},{2,0},{3,1},{4,6},{5,7},{6,4},{7,5},{8,10},{9,11},{10,... | collective-permute-start | bytes 1179656 | tf_op jit(solution)/shard_map/ppermute | solution.py:462
  (82 other events, 717.4 us)
